TPU v7x, 256 devices: a whole 4x4x8 slice. The times are simulated.
256 devices in a mesh: dp: 2 (over core), seq: 8 (over z), expert: 16 (over y, x).
Axes of the slice: x: 4, y: 4, z: 8, core: 2. Of those that a mesh axis runs over, the one named last changes fastest.
Arguments:
- tokens: bfloat16 [16384, 2048], P(('dp', 'seq')), may hold values from -6 to 6
- phi: bfloat16 [2048, 32], P(None, 'expert'), may hold values from -40 to 40
- w_in: bfloat16 [32, 2048, 8192], P('expert', None, ('dp', 'seq')), may hold values from -1 to 1
- w_out: bfloat16 [32, 8192, 2048], P('expert', ('dp', 'seq')), may hold values from -0.25 to 0.25
Outputs:
- mixed: bfloat16 [16384, 2048], P(('dp', 'seq', 'expert'))
All inputs are finite; a program needn't handle non-finite values.
Results may differ from a plain program's by a relative error of at most 0.0068.
Values may be sent and summed in bfloat16 or wider, within the bound.
A program may use at most 64 MiB of HBM per device.

v0:
```python
import jax
import jax.numpy as jnp
from jax import lax
from jax.sharding import PartitionSpec as P


def on_device(tokens, phi, w_in, w_out):
    n_expert = lax.axis_size("expert")
    rows_out = tokens.shape[0] // n_expert
    phi_all = lax.all_gather(phi, "expert", axis=1, tiled=True)
    logits = lax.dot_general(
        phi, tokens, (((0,), (1,)), ((), ())), preferred_element_type=jnp.float32
    )
    slot_max = lax.pmax(jnp.max(logits, axis=1), "seq")
    spread = jnp.exp(logits - slot_max[:, None])
    numerator = jnp.dot(spread.astype(jnp.bfloat16), tokens, preferred_element_type=jnp.float32)
    denominator = jnp.sum(spread, axis=1)
    numer_seq, denom_seq = lax.psum((numerator, denominator), "seq")
    own_slots = (numer_seq / denom_seq[:, None]).astype(jnp.bfloat16)
    slot_in = lax.all_gather(own_slots[None], "dp", axis=0, tiled=True)
    hidden = jax.nn.gelu(
        jnp.einsum("ced,edf->cef", slot_in, w_in, preferred_element_type=jnp.float32),
        approximate=True,
    ).astype(jnp.bfloat16)
    partial_value = jnp.einsum("cef,efd->ced", hidden, w_out, preferred_element_type=jnp.float32)
    totals = lax.psum(partial_value, ("dp", "seq"))
    summed = lax.dynamic_index_in_dim(totals, lax.axis_index("dp"), 0, keepdims=False)
    slot_out = lax.all_gather(summed.astype(jnp.bfloat16), "expert", axis=0, tiled=True)
    rows = lax.dynamic_slice_in_dim(tokens, lax.axis_index("expert") * rows_out, rows_out, 0)
    row_logits = lax.dot_general(
        phi_all, rows, (((0,), (1,)), ((), ())), preferred_element_type=jnp.float32
    )
    row_max = jnp.max(row_logits, axis=0)
    combine_weights = jnp.exp(row_logits - row_max[None, :])
    mixed_numer = lax.dot_general(
        combine_weights.astype(jnp.bfloat16),
        slot_out,
        (((0,), (0,)), ((), ())),
        preferred_element_type=jnp.float32,
    )
    mixed_denom = jnp.sum(combine_weights, axis=0)
    return (mixed_numer / mixed_denom[:, None]).astype(jnp.bfloat16)


def solution(mesh):
    placed = (
        P(("dp", "seq"), None),
        P(None, "expert"),
        P("expert", None, ("dp", "seq")),
        P("expert", ("dp", "seq"), None),
    )
    return jax.shard_map(
        on_device,
        mesh=mesh,
        in_specs=placed,
        out_specs=P(("dp", "seq", "expert"), None),
        check_vma=False,
    )
```

profile of v0, /device:TPU:32, one launch (start us, length us, event | category | flops | bytes accessed | tf_op | source)
XLA Modules:
  0.0 159.4 jit_solution(6288700102996713554)
XLA Ops:
  0.0 3.5 %fusion.39 = (f32[2]{0:T(128)S(1)}, f32[2,1024]{1,0:T(2,128)S(1)}) fusion(bf16[2048,2]{0,1:T(2,128)(2,1)} %param.5, bf16[1024,2048]{1,0:T(8,128)(2,1)} %param.4), kind=kOutput, calls=%fused_computation.39 | convolution fusion | flops 8390654 | bytes 4210696 | tf_op jit(solution)/shard_map/dot_general | solution.py:11
  3.5 17.9 %pmax.7 = f32[2]{0:T(128)S(1)} all-reduce(f32[2]{0:T(128)S(1)} %get-tuple-element.9), channel_id=1, replica_groups=mesh['dp'=2,'seq'=8,'expert'=16] {'seq'}, use_global_device_ids=true, to_apply=%region_2.0 | all-reduce | flops 2 | bytes 16 | tf_op jit(solution)/shard_map/pmax | solution.py:14
  21.4 0.2 fusion.25
  21.6 2.9 %fusion.27 = f32[2,2048]{1,0:T(2,128)S(1)} fusion(bf16[1024,2048]{1,0:T(8,128)(2,1)} %param.4, f32[2,1024]{1,0:T(2,128)S(1)} %get-tuple-element.10, f32[2]{0:T(128)S(1)} %pmax.7), kind=kOutput, calls=%fused_computation.28 | convolution fusion | flops 8392704 | bytes 4218888 | tf_op jit(solution)/shard_map/dot_general | solution.py:16
  24.5 27.9 %all-reduce = (f32[2,2048]{1,0:T(2,128)S(1)}, f32[2]{0:T(128)S(1)}) all-reduce(f32[2,2048]{1,0:T(2,128)S(1)} %fusion.27, f32[2]{0:T(128)S(1)} %fusion.25), channel_id=1, replica_groups=mesh['dp'=2,'seq'=8,'expert'=16] {'seq'}, use_global_device_ids=true, to_apply=%region_3.0 | all-reduce | flops 4098 | bytes 32784 | tf_op jit(solution)/shard_map/psum | solution.py:18
  52.4 0.1 fusion.24
  52.5 1.8 %all-gather.3 = bf16[2,2,2048]{2,1,0:T(2,128)(2,1)S(1)} all-gather(bf16[1,2,2048]{2,1,0:T(2,128)(2,1)S(1)} %fusion.24), channel_id=2, replica_groups=mesh['dp'=2,'seq'=8,'expert'=16] {'dp'}, dimensions={0}, use_global_device_ids=true | all-gather | bytes 24576 | tf_op jit(solution)/shard_map/all_gather | solution.py:20
  54.3 0.0 copy-start
  54.3 4.7 %convolution_bitcast_fusion = f32[2,2,2048]{2,0,1:T(2,128)S(1)} fusion(bf16[2,512,2048]{2,1,0:T(8,128)(2,1)} %param.7, bf16[2,2048,512]{2,1,0:T(8,128)(2,1)} %param.6, bf16[2,2,2048]{2,1,0:T(2,128)(2,1)S(1)} %all-gather.3), kind=kOutput, calls=%fused_computation.2 | convolution fusion | flops 16795648 | bytes 8437760 | tf_op jit(solution)/shard_map/cef,efd->ced/dot_general | solution.py:25
  59.0 51.1 %psum.23 = bf16[2,2,2048]{2,0,1:T(2,128)(2,1)S(1)} all-reduce(f32[2,2,2048]{2,0,1:T(2,128)S(1)} %convolution_bitcast_fusion), channel_id=1, replica_groups=mesh['dp'=2,'seq'=8,'expert'=16] {'dp','seq'}, use_global_device_ids=true, to_apply=%region_6.7 | all-reduce | flops 8192 | bytes 49152 | tf_op jit(solution)/shard_map/psum | solution.py:26
  110.1 0.0 copy-done
  110.1 24.0 %all-gather.2 = bf16[16,2,2048]{2,1,0:T(2,128)(2,1)S(1)} all-gather(bf16[1,2,2048]{2,1,0:T(2,128)(2,1)S(1)} %bitcast.24), channel_id=1, replica_groups=mesh['dp'=2,'seq'=8,'expert'=16] {'expert'}, dimensions={0}, use_global_device_ids=true | all-gather | bytes 139264 | tf_op jit(solution)/shard_map/all_gather | solution.py:10
  134.1 0.1 reshape.8
  134.1 1.2 fusion.38
  135.3 23.1 %all-gather.1 = bf16[1,32,2048]{2,0,1:T(2,128)(2,1)S(1)} all-gather(bf16[1,2,2048]{2,0,1:T(2,128)(2,1)S(1)} %dynamic-slice_convert_fusion), channel_id=3, replica_groups=mesh['dp'=2,'seq'=8,'expert'=16] {'expert'}, dimensions={1}, use_global_device_ids=true | all-gather | bytes 139264 | tf_op jit(solution)/shard_map/all_gather | solution.py:28
  158.4 1.0 fusion
  (2 shorter events, 0.1 us)
Async XLA Ops:
  54.3 55.8 %copy-start = (bf16[2048,2]{0,1:T(2,128)(2,1)S(1)}, bf16[2048,2]{0,1:T(2,128)(2,1)}, u32[]{:S(2)}) copy-start(bf16[2048,2]{0,1:T(2,128)(2,1)} %param.5) | copy-start | bytes 24580
where the time goes:
time: 160 us; the launch traced here: 159 us
  blocking collectives  146 us (91%)
  matrix products  13.2 us (8%)
    psum x1, blocking collectives, on_device(): totals = lax.psum(partial_value, ('dp', 'seq'))  51.1 us
    psum x1, blocking collectives, on_device(): numer_seq, denom_seq = lax.psum((numerator, denominator), 'seq')  27.9 us
    all_gather x1, blocking collectives, on_device(): phi_all = lax.all_gather(phi, 'expert', axis=1, tiled=True)  24 us
    all_gather x1, blocking collectives, on_device(): lax.all_gather(summed.astype(jnp.bfloat16), 'expert', axis=0, tiled=True)  23.1 us
    pmax x1, blocking collectives, on_device(): slot_max = lax.pmax(jnp.max(logits, axis=1), 'seq')  17.9 us
    dot_general x1, matrix products, on_device(): jnp.einsum('cef,efd->ced', hidden, w_out, preferred_element_type=jnp.floa...  4.66 us
    dot_general x1, matrix products, on_device(): lax.dot_general(phi, tokens, (((0,), (1,)), ((), ())), preferred_element_...  3.5 us

commit v1 on v0

--- a/solution.py
+++ b/solution.py
@@ -25,7 +25,12 @@
     partial_value = jnp.einsum("cef,efd->ced", hidden, w_out, preferred_element_type=jnp.float32)
     totals = lax.psum(partial_value, ("dp", "seq"))
     summed = lax.dynamic_index_in_dim(totals, lax.axis_index("dp"), 0, keepdims=False)
-    slot_out = lax.all_gather(summed.astype(jnp.bfloat16), "expert", axis=0, tiled=True)
+    slot_out = jnp.concatenate(
+        lax.all_to_all(
+            jnp.stack([summed.astype(jnp.bfloat16)] * lax.psum(1, "expert")), "expert", 0, 0
+        ),
+        axis=0,
+    )
     rows = lax.dynamic_slice_in_dim(tokens, lax.axis_index("expert") * rows_out, rows_out, 0)
     row_logits = lax.dot_general(
         phi_all, rows, (((0,), (1,)), ((), ())), preferred_element_type=jnp.float32

time: 160 us -> 145 us (0.906)
  blocking collectives: 146 us -> 123 us
  starting transfers between devices: 0 us -> 7.03 us
    all_gather x1 -> x0, blocking collectives: 23.1 us -> none  [on_device(): lax.all_gather(summed.astype(jnp.bfloat16), 'expert', axis=0, tiled=True)]
    all_to_all x0 -> x1, starting transfers between devices: none -> 7.03 us  [on_device(): lax.all_to_all(jnp.stack([summed.astype(jnp.bfloat16)] * lax.psum(1, 'exp...]
  transfers between devices with their start and end apart: 0 -> 1, of which waited for: 0 -> 0; matrix products, arithmetic and copies ran while one was open for 0% -> 1% of each run, Pallas kernels for 0% -> 0%
where the time goes in v1:
time: 145 us; the launch traced here: 144 us
  blocking collectives  123 us (85%)
  matrix products  13.2 us (9%)
  starting transfers between devices  7.03 us (5%)
    psum x1, blocking collectives, on_device(): totals = lax.psum(partial_value, ('dp', 'seq'))  51.1 us
    psum x1, blocking collectives, on_device(): numer_seq, denom_seq = lax.psum((numerator, denominator), 'seq')  27.9 us
    all_gather x1, blocking collectives, on_device(): phi_all = lax.all_gather(phi, 'expert', axis=1, tiled=True)  24.1 us
    pmax x1, blocking collectives, on_device(): slot_max = lax.pmax(jnp.max(logits, axis=1), 'seq')  17.9 us
    all_to_all x1, starting transfers between devices, on_device(): lax.all_to_all(jnp.stack([summed.astype(jnp.bfloat16)] * lax.psum(1, 'exp...  7.03 us
    dot_general x1, matrix products, on_device(): jnp.einsum('cef,efd->ced', hidden, w_out, preferred_element_type=jnp.floa...  4.66 us
    dot_general x1, matrix products, on_device(): lax.dot_general(phi, tokens, (((0,), (1,)), ((), ())), preferred_element_...  3.5 us
  transfers between devices with their start and end apart: 1, of which 0 were waited for; matrix products, arithmetic and copies ran while one was open for 1% of the time, Pallas kernels for 0%

profile of v1, /device:TPU:32, one launch (start us, length us, event | category | flops | bytes accessed | tf_op | source)
XLA Modules:
  0.0 144.3 jit_solution(3198205607291277104)
XLA Ops:
  0.0 3.5 %fusion.36 = (f32[2]{0:T(128)S(1)}, f32[2,1024]{1,0:T(2,128)S(1)}) fusion(bf16[2048,2]{0,1:T(2,128)(2,1)} %param.5, bf16[1024,2048]{1,0:T(8,128)(2,1)} %param.4), kind=kOutput, calls=%fused_computation.37 | convolution fusion | flops 8390654 | bytes 4210696 | tf_op jit(solution)/shard_map/dot_general | solution.py:11
  3.5 17.9 %pmax.7 = f32[2]{0:T(128)S(1)} all-reduce(f32[2]{0:T(128)S(1)} %get-tuple-element.7), channel_id=1, replica_groups=mesh['dp'=2,'seq'=8,'expert'=16] {'seq'}, use_global_device_ids=true, to_apply=%region_2.0 | all-reduce | flops 2 | bytes 16 | tf_op jit(solution)/shard_map/pmax | solution.py:14
  21.4 0.2 fusion.23
  21.6 2.9 %fusion.25 = f32[2,2048]{1,0:T(2,128)S(1)} fusion(bf16[1024,2048]{1,0:T(8,128)(2,1)} %param.4, f32[2,1024]{1,0:T(2,128)S(1)} %get-tuple-element.8, f32[2]{0:T(128)S(1)} %pmax.7), kind=kOutput, calls=%fused_computation.27 | convolution fusion | flops 8392704 | bytes 4218888 | tf_op jit(solution)/shard_map/dot_general | solution.py:16
  24.5 27.9 %all-reduce = (f32[2,2048]{1,0:T(2,128)S(1)}, f32[2]{0:T(128)S(1)}) all-reduce(f32[2,2048]{1,0:T(2,128)S(1)} %fusion.25, f32[2]{0:T(128)S(1)} %fusion.23), channel_id=1, replica_groups=mesh['dp'=2,'seq'=8,'expert'=16] {'seq'}, use_global_device_ids=true, to_apply=%region_3.0 | all-reduce | flops 4098 | bytes 32784 | tf_op jit(solution)/shard_map/psum | solution.py:18
  52.4 0.1 fusion.22
  52.5 1.8 %all-gather.2 = bf16[2,2,2048]{2,1,0:T(2,128)(2,1)S(1)} all-gather(bf16[1,2,2048]{2,1,0:T(2,128)(2,1)S(1)} %fusion.22), channel_id=2, replica_groups=mesh['dp'=2,'seq'=8,'expert'=16] {'dp'}, dimensions={0}, use_global_device_ids=true | all-gather | bytes 24576 | tf_op jit(solution)/shard_map/all_gather | solution.py:20
  54.3 0.0 copy-start
  54.3 4.7 %convolution_bitcast_fusion = f32[2,2,2048]{2,0,1:T(2,128)S(1)} fusion(bf16[2,512,2048]{2,1,0:T(8,128)(2,1)} %param.7, bf16[2,2048,512]{2,1,0:T(8,128)(2,1)} %param.6, bf16[2,2,2048]{2,1,0:T(2,128)(2,1)S(1)} %all-gather.2), kind=kOutput, calls=%fused_computation.2 | convolution fusion | flops 16795648 | bytes 8437760 | tf_op jit(solution)/shard_map/cef,efd->ced/dot_general | solution.py:25
  59.0 51.1 %psum.23 = bf16[2,2,2048]{2,0,1:T(2,128)(2,1)S(1)} all-reduce(f32[2,2,2048]{2,0,1:T(2,128)S(1)} %convolution_bitcast_fusion), channel_id=1, replica_groups=mesh['dp'=2,'seq'=8,'expert'=16] {'dp','seq'}, use_global_device_ids=true, to_apply=%region_6.7 | all-reduce | flops 8192 | bytes 49152 | tf_op jit(solution)/shard_map/psum | solution.py:26
  110.1 0.7 stack.5
  110.8 7.0 %all-to-all-start = ((bf16[16,2,2048]{2,1,0:T(2,128)(2,1)}), bf16[16,2,2048]{2,1,0:T(2,128)(2,1)S(1)}, u32[]{:S(2)}, u32[]{:S(2)}) async-start(bf16[16,2,2048]{2,1,0:T(2,128)(2,1)} %stack.5), calls=%async_computation | async-start | bytes 262144 | tf_op jit(solution)/shard_map/all_to_all | solution.py:29
  117.9 0.0 copy-done
  117.9 24.1 %all-gather.1 = bf16[16,2,2048]{2,1,0:T(2,128)(2,1)S(1)} all-gather(bf16[1,2,2048]{2,1,0:T(2,128)(2,1)S(1)} %bitcast.25), channel_id=1, replica_groups=mesh['dp'=2,'seq'=8,'expert'=16] {'expert'}, dimensions={0}, use_global_device_ids=true | all-gather | bytes 139264 | tf_op jit(solution)/shard_map/all_gather | solution.py:10
  142.0 0.1 reshape.11
  142.0 1.2 fusion.37
  143.2 0.0 all-to-all-done
  143.2 0.1 reshape.8
  143.3 1.0 fusion
  (3 shorter events, 0.1 us)
Async XLA Ops:
  54.3 63.6 %copy-start = (bf16[2048,2]{0,1:T(2,128)(2,1)S(1)}, bf16[2048,2]{0,1:T(2,128)(2,1)}, u32[]{:S(2)}) copy-start(bf16[2048,2]{0,1:T(2,128)(2,1)} %param.5) | copy-start | bytes 24580
  110.8 32.4 %all-to-all-start = ((bf16[16,2,2048]{2,1,0:T(2,128)(2,1)}), bf16[16,2,2048]{2,1,0:T(2,128)(2,1)S(1)}, u32[]{:S(2)}, u32[]{:S(2)}) async-start(bf16[16,2,2048]{2,1,0:T(2,128)(2,1)} %stack.5), calls=%async_computation | async-start | bytes 262144 | tf_op jit(solution)/shard_map/all_to_all | solution.py:29
